TPU v7x, 512 devices: a whole 4x4x16 slice. The times are simulated.
512 devices in a mesh: space: 32 (over x, y, core), vel: 16 (over z).
Axes of the slice: x: 4, y: 4, z: 16, core: 2. Of those that a mesh axis runs over, the one named last changes fastest.
Arguments:
- distribution: float32 [4096, 32768], P('vel', 'space'), may hold values from -48 to 48
- kernel: bfloat16 [4096, 4096], P('vel'), may hold values from -0.046875 to 0.046875
- frequency: float32 [4096], P('vel'), may hold values from 0.05 to 0.5
- accommodation: float32 [8], replicated, may hold values from 0.2 to 0.95
- wall_class: int32 [2, 1024], P(None, 'space'), may hold values from 0 to 7
Outputs:
- updated: float32 [4096, 32768], P('vel', 'space')
All inputs are finite; a program needn't handle non-finite values.
Results may differ from a plain program's by a relative error of at most 0.0018.
Values may be sent and summed in bfloat16 or wider, within the bound.
No kernel may reach another device: no remote copies, remote signals or barrier semaphores. Data moves between devices by JAX's collectives and lax.ppermute only.
A program may use at most 64 MiB of HBM per device.

v0:
```python
import jax
import jax.numpy as jnp
from jax import lax
from jax.sharding import PartitionSpec as P

NV1 = 16
NY = 32
NCLASS = 8


courant_x = 0.05
courant_y = 0.15


def swapped(value, axis, distance):
    return lax.ppermute(value, axis, [(i, i ^ 1 << distance) for i in range(lax.axis_size(axis))])


def extended(value, sides, width):
    for axis, dim in sides:
        devices, length = (lax.axis_size(axis), value.shape[dim])
        up = [(i, (i + 1) % devices) for i in range(devices)]
        down = [(j, i) for i, j in up]
        last = lax.slice_in_dim(value, length - width, length, axis=dim)
        initial = lax.slice_in_dim(value, 0, width, axis=dim)
        before = lax.ppermute(last, axis, up)
        after = lax.ppermute(initial, axis, down)
        value = jnp.concatenate([before, value, after], axis=dim)
    return value


def velocity_parts(vel_index):
    spacing = 9.6 / NV1
    middle = (NV1 - 1) / 2.0
    index_y = vel_index // (NV1 * NV1)
    index_x = vel_index // NV1 % NV1
    index_z = vel_index % NV1
    vel_x = (index_x.astype(jnp.float32) - middle) * spacing
    vel_y = (index_y.astype(jnp.float32) - middle) * spacing
    vel_z = (index_z.astype(jnp.float32) - middle) * spacing
    return (vel_x, vel_y, vel_z)


def grid_constants():
    spacing = 9.6 / NV1
    middle = (NV1 - 1) / 2.0
    points = (lax.iota(jnp.int32, NV1).astype(jnp.float32) - middle) * spacing
    weights = jnp.exp(-0.5 * points * points)
    zsum = jnp.sum(weights)
    outflow = jnp.sum(jnp.where(points > 0, points * weights, 0.0)) / zsum
    return (zsum * zsum * zsum, outflow)


def per_device(distribution, kernel, frequency, accommodation, wall_class):
    vel_rows, cell_count = distribution.shape
    rank = lax.axis_index("vel")
    vel_index = rank * vel_rows + lax.iota(jnp.int32, vel_rows)
    vel_x, vel_y, vel_z = velocity_parts(vel_index)
    normal_sum, outflow = grid_constants()
    maxwell = jnp.exp(-0.5 * (vel_x * vel_x + vel_y * vel_y + vel_z * vel_z)) / normal_sum
    lowered = distribution.astype(jnp.bfloat16)
    walls = jnp.stack([lowered[:, 0::NY], lowered[:, NY - 1 :: NY]])
    wide = walls.astype(jnp.float32)
    down_weight = jnp.where(vel_y < 0, -vel_y, 0.0)
    up_weight = jnp.where(vel_y > 0, vel_y, 0.0)
    partial_flux = jnp.stack(
        [
            jnp.sum(down_weight[:, None] * wide[0], axis=0),
            jnp.sum(up_weight[:, None] * wide[1], axis=0),
        ]
    )
    flux = lax.psum(partial_flux, "vel")
    mirrored = walls
    log_rows = vel_rows.bit_length() - 1
    log_devices = lax.axis_size("vel").bit_length() - 1
    log_plane = 2 * (NV1.bit_length() - 1)
    for bit_index in range(max(log_plane - log_rows, 0), log_devices):
        mirrored = swapped(mirrored, "vel", bit_index)
    mirrored = mirrored.astype(jnp.float32)
    sigma = flux / outflow
    class_ids = lax.iota(jnp.int32, NCLASS)
    alpha = jnp.sum(
        jnp.where(
            wall_class[:, :, None] == class_ids[None, None, :], accommodation[None, None, :], 0.0
        ),
        axis=2,
    )
    inflow = (
        alpha[:, None, :] * sigma[:, None, :] * maxwell[None, :, None]
        + (1.0 - alpha)[:, None, :] * mirrored
    )
    padded = extended(distribution.astype(jnp.bfloat16), (("space", 1),), NY).astype(
        distribution.dtype
    )
    left = padded[:, :cell_count]
    right = padded[:, 2 * NY :]
    y_place = lax.iota(jnp.int32, cell_count) % NY
    below = jnp.concatenate([distribution[:, :1], distribution[:, :-1]], axis=1)
    below = jnp.where(y_place[None, :] == 0, jnp.repeat(inflow[0], NY, axis=1), below)
    above = jnp.concatenate([distribution[:, 1:], distribution[:, -1:]], axis=1)
    above = jnp.where(y_place[None, :] == NY - 1, jnp.repeat(inflow[1], NY, axis=1), above)
    move_x = courant_x * (
        jnp.maximum(vel_x, 0.0)[:, None] * (distribution - left)
        + jnp.minimum(vel_x, 0.0)[:, None] * (right - distribution)
    )
    move_y = courant_y * (
        jnp.maximum(vel_y, 0.0)[:, None] * (distribution - below)
        + jnp.minimum(vel_y, 0.0)[:, None] * (above - distribution)
    )
    moved = move_x + move_y
    shard_piece = lax.all_gather(lowered, "vel", axis=0, tiled=True)
    running = jnp.dot(kernel, shard_piece, preferred_element_type=jnp.float32)
    piece_walls = jnp.stack([shard_piece[:, 0::NY], shard_piece[:, NY - 1 :: NY]])
    wall_store = piece_walls
    gain, wall_store = (running, wall_store)
    return distribution - moved - frequency[:, None] * distribution + gain


def solution(mesh):
    placed = (P("vel", "space"), P("vel", None), P("vel"), P(), P(None, "space"))
    return jax.shard_map(
        per_device, mesh=mesh, in_specs=placed, out_specs=P("vel", "space"), check_vma=False
    )
```

profile of v0, /device:TPU:2, one launch (start us, length us, event | category | flops | bytes accessed | tf_op | source)
XLA Modules:
  0.0 138.9 jit_solution(6166455411923694393)
XLA Ops:
  6.5 0.0 all-gather.2.cloned.1.call-start
  6.6 2.3 %convert_element_type.60 = bf16[256,1024]{1,0:T(8,128)(2,1)} convert(f32[256,1024]{1,0:T(8,128)} %param.5) | non-fusion elementwise | flops 262144 | bytes 1572864 | tf_op jit(solution)/shard_map/convert_element_type | solution.py:92
  8.9 1.7 %slice.47 = bf16[256,32]{1,0:T(8,128)(2,1)S(1)} slice(bf16[256,1024]{1,0:T(8,128)(2,1)} %convert_element_type.60), slice={[0:256:1], [31:1024:32]} | slice | bytes 32768 | tf_op jit(solution)/shard_map/slice | solution.py:62
  10.6 1.7 %slice.46 = bf16[256,32]{1,0:T(8,128)(2,1)S(1)} slice(bf16[256,1024]{1,0:T(8,128)(2,1)} %convert_element_type.60), slice={[0:256:1], [0:1024:32]} | slice | bytes 32768 | tf_op jit(solution)/shard_map/slice | solution.py:62
  12.3 0.1 copy.15
  12.3 0.1 copy.14
  12.4 3.8 %collective-permute-start.2 = (bf16[2,256,32]{1,2,0:T(8,128)(2,1)S(1)}, bf16[2,256,32]{1,2,0:T(8,128)(2,1)}, u32[]{:S(2)}, u32[]{:S(2)}) collective-permute-start(bf16[2,256,32]{1,2,0:T(8,128)(2,1)S(1)} %get-tuple-element.16), channel_id=1, source_target_pairs={{0,1},{1,0},{2,3},{3,2},{4,5},{5,4},{6,7},{7,6},{8,9},{9,8},{10,11... | collective-permute-start | bytes 98312 | tf_op jit(solution)/shard_map/ppermute | solution.py:16
  16.3 1.6 %fusion.35 = (bf16[256,32]{1,0:T(8,128)(2,1)}, bf16[256,32]{1,0:T(8,128)(2,1)}) fusion(bf16[256,1024]{1,0:T(8,128)(2,1)} %convert_element_type.60), kind=kLoop, calls=%fused_computation.78 | loop fusion | bytes 65536 | tf_op jit(solution)/shard_map/slice | solution.py:25
  17.9 4.0 %collective-permute-start.1 = (bf16[256,32]{1,0:T(8,128)(2,1)}, bf16[256,32]{1,0:T(8,128)(2,1)S(1)}, u32[]{:S(2)}, u32[]{:S(2)}) collective-permute-start(bf16[256,32]{1,0:T(8,128)(2,1)} %get-tuple-element.11), channel_id=1, source_target_pairs={{16,0},{32,16},{48,32},{64,48},{80,64},{96,80},{112,96},{128,112},... | collective-permute-start | bytes 49160 | tf_op jit(solution)/shard_map/ppermute | solution.py:27
  21.9 1.9 %collective-permute-start = (bf16[256,32]{1,0:T(8,128)(2,1)}, bf16[256,32]{1,0:T(8,128)(2,1)}, u32[]{:S(2)}, u32[]{:S(2)}) collective-permute-start(bf16[256,32]{1,0:T(8,128)(2,1)} %get-tuple-element.12), channel_id=1, source_target_pairs={{0,16},{16,32},{32,48},{48,64},{64,80},{80,96},{96,112},{112,128},... | collective-permute-start | bytes 49160 | tf_op jit(solution)/shard_map/ppermute | solution.py:26
  23.8 0.6 fusion.31
  24.5 0.6 fusion.29
  26.3 0.1 fusion.16
  26.4 36.6 %psum.7 = f32[2,32]{1,0:T(2,128)S(1)} all-reduce(f32[2,32]{1,0:T(2,128)S(1)} %pad_maximum_fusion.1), channel_id=1, replica_groups=mesh['space'=32,'vel'=16] {'vel'}, use_global_device_ids=true, to_apply=%region_3.4 | all-reduce | flops 64 | bytes 512 | tf_op jit(solution)/shard_map/psum | solution.py:72
  63.0 0.1 select_reduce_fusion
  63.1 0.1 fusion.34
  63.2 1.7 %fusion.33 = (f32[256,1023]{1,0:T(8,128)}, f32[256,1023]{1,0:T(8,128)}) fusion(f32[256,1024]{1,0:T(8,128)S(1)} %copy-done.1), kind=kLoop, calls=%fused_computation.76 | loop fusion | bytes 4190208 | tf_op jit(solution)/shard_map/slice | solution.py:100
  64.9 2.2 %collective-permute-start.3 = (bf16[2,256,32]{1,2,0:T(8,128)(2,1)}, bf16[2,256,32]{1,2,0:T(8,128)(2,1)S(1)}, u32[]{:S(2)}, u32[]{:S(2)}) collective-permute-start(bf16[2,256,32]{1,2,0:T(8,128)(2,1)} %collective-permute-done.2), channel_id=1, source_target_pairs={{0,2},{1,3},{2,0},{3,1},{4,6},{5,7},{6,4},{7,5},{8,10},{9,11},{10,... | collective-permute-start | bytes 98312 | tf_op jit(solution)/shard_map/ppermute | solution.py:16
  67.1 5.7 %collective-permute-done.3 = bf16[2,256,32]{1,2,0:T(8,128)(2,1)S(1)} collective-permute-done((bf16[2,256,32]{1,2,0:T(8,128)(2,1)}, bf16[2,256,32]{1,2,0:T(8,128)(2,1)S(1)}, u32[]{:S(2)}, u32[]{:S(2)}) %collective-permute-start.3) | collective-permute-done | bytes 32800 | tf_op jit(solution)/shard_map/ppermute | solution.py:16
  72.8 3.7 %collective-permute-start.4 = (bf16[2,256,32]{1,2,0:T(8,128)(2,1)S(1)}, bf16[2,256,32]{1,2,0:T(8,128)(2,1)}, u32[]{:S(2)}, u32[]{:S(2)}) collective-permute-start(bf16[2,256,32]{1,2,0:T(8,128)(2,1)S(1)} %collective-permute-done.3), channel_id=1, source_target_pairs={{0,4},{1,5},{2,6},{3,7},{4,0},{5,1},{6,2},{7,3},{8,12},{9,13},{10,... | collective-permute-start | bytes 98312 | tf_op jit(solution)/shard_map/ppermute | solution.py:16
  78.4 5.7 %collective-permute-done.4 = bf16[2,256,32]{1,2,0:T(8,128)(2,1)} collective-permute-done((bf16[2,256,32]{1,2,0:T(8,128)(2,1)S(1)}, bf16[2,256,32]{1,2,0:T(8,128)(2,1)}, u32[]{:S(2)}, u32[]{:S(2)}) %collective-permute-start.4) | collective-permute-done | bytes 32800 | tf_op jit(solution)/shard_map/ppermute | solution.py:16
  84.0 8.3 %collective-permute-start.5 = (bf16[2,256,32]{1,2,0:T(8,128)(2,1)}, bf16[2,256,32]{1,2,0:T(8,128)(2,1)S(1)}, u32[]{:S(2)}, u32[]{:S(2)}) collective-permute-start(bf16[2,256,32]{1,2,0:T(8,128)(2,1)} %collective-permute-done.4), channel_id=1, source_target_pairs={{0,8},{1,9},{2,10},{3,11},{4,12},{5,13},{6,14},{7,15},{8,0},{9,1},... | collective-permute-start | bytes 98312 | tf_op jit(solution)/shard_map/ppermute | solution.py:16
  92.4 2.2 %concatenate.9 = bf16[256,1088]{1,0:T(8,128)(2,1)} concatenate(bf16[256,32]{1,0:T(8,128)(2,1)} %collective-permute-done, bf16[256,1024]{1,0:T(8,128)(2,1)} %convert_element_type.60, bf16[256,32]{1,0:T(8,128)(2,1)S(1)} %collective-permute-done.1), dimensions={1} | concatenate | bytes 1114112 | tf_op jit(solution)/shard_map/concatenate | solution.py:28
  94.6 2.3 %convert_element_type.61 = f32[256,1088]{1,0:T(8,128)} convert(bf16[256,1088]{1,0:T(8,128)(2,1)} %concatenate.9) | non-fusion elementwise | flops 278528 | bytes 1671168 | tf_op jit(solution)/shard_map/convert_element_type | solution.py:92
  96.8 2.8 %collective-permute-done.5 = bf16[2,256,32]{1,2,0:T(8,128)(2,1)S(1)} collective-permute-done((bf16[2,256,32]{1,2,0:T(8,128)(2,1)}, bf16[2,256,32]{1,2,0:T(8,128)(2,1)S(1)}, u32[]{:S(2)}, u32[]{:S(2)}) %collective-permute-start.5) | collective-permute-done | bytes 32800 | tf_op jit(solution)/shard_map/ppermute | solution.py:16
  99.6 0.1 multiply_add_fusion
  99.7 1.1 broadcast_in_dim.57
  100.7 2.6 %copy.17 = f32[256,1024]{1,0:T(8,128)} copy(f32[256,1024]{0,1:T(8,128)} %bitcast.24) | data formatting | bytes 2097152 | tf_op jit(solution)/shard_map/reshape | solution.py:101
  103.4 1.1 broadcast_in_dim.55
  104.4 2.6 %copy.16 = f32[256,1024]{1,0:T(8,128)} copy(f32[256,1024]{0,1:T(8,128)} %bitcast.25) | data formatting | bytes 2097152 | tf_op jit(solution)/shard_map/reshape | solution.py:99
  107.0 16.7 %all-gather.2.cloned.1.call-done = bf16[4096,1024]{1,0:T(8,128)(2,1)} async-done(((bf16[256,1024]{1,0:T(8,128)(2,1)}), bf16[4096,1024]{1,0:T(8,128)(2,1)}) %all-gather.2.cloned.1.call-update) | async-done | bytes 8388624 | tf_op jit(solution)/shard_map/all_gather | solution.py:111
  123.7 8.4 %convolution_add_fusion = f32[256,1024]{1,0:T(8,128)} fusion(bf16[256,4096]{1,0:T(8,128)(2,1)S(1)} %copy-done, bf16[4096,1024]{1,0:T(8,128)(2,1)} %all-gather.2.cloned.1.call-done, f32[256,1024]{1,0:T(8,128)S(1)} %copy-done.1, f32[256,1088]{1,0:T(8,128)} %convert_element_type.61, f32[256,1024]{1,0:T(8,128)} %copy.16, f32[256,1023]{1,0:T(8,128)} %get-tuple-element.8, ...), kind=kOutput, calls=%fused_computation | convolution fusion | flops 2152988672 | bytes 18881536 | tf_op jit(solution)/shard_map/dot_general | solution.py:112
  (23 shorter events, 0.2 us)
Async XLA Ops:
  6.5 117.1 %copy-start = (bf16[256,4096]{1,0:T(8,128)(2,1)S(1)}, bf16[256,4096]{1,0:T(8,128)(2,1)}, u32[]{:S(2)}) copy-start(bf16[256,4096]{1,0:T(8,128)(2,1)} %param.6) | copy-start | bytes 6291460
  6.5 56.6 %copy-start.1 = (f32[256,1024]{1,0:T(8,128)S(1)}, f32[256,1024]{1,0:T(8,128)}, u32[]{:S(2)}) copy-start(f32[256,1024]{1,0:T(8,128)} %param.5) | copy-start | bytes 3145732
  6.5 56.5 %copy-start.2 = (s32[2,32]{1,0:T(2,128)S(1)}, s32[2,32]{1,0:T(2,128)}, u32[]{:S(2)}) copy-start(s32[2,32]{1,0:T(2,128)} %param.9) | copy-start | bytes 772
  6.5 56.5 %copy-start.3 = (f32[8]{0:T(128)S(1)}, f32[8]{0:T(128)}, u32[]{:S(2)}) copy-start(f32[8]{0:T(128)} %param.8) | copy-start | bytes 100
  6.5 117.1 %all-gather.2.cloned.1.call-start = ((), (), s32[]{:S(2)}) async-start(), calls=%async_computation | async-start | bytes 8912896 | tf_op jit(solution)/shard_map/all_gather | solution.py:111
  12.4 52.5 %collective-permute-start.2 = (bf16[2,256,32]{1,2,0:T(8,128)(2,1)S(1)}, bf16[2,256,32]{1,2,0:T(8,128)(2,1)}, u32[]{:S(2)}, u32[]{:S(2)}) collective-permute-start(bf16[2,256,32]{1,2,0:T(8,128)(2,1)S(1)} %get-tuple-element.16), channel_id=1, source_target_pairs={{0,1},{1,0},{2,3},{3,2},{4,5},{5,4},{6,7},{7,6},{8,9},{9,8},{10,11... | collective-permute-start | bytes 98312 | tf_op jit(solution)/shard_map/ppermute | solution.py:16
  17.9 74.5 %collective-permute-start.1 = (bf16[256,32]{1,0:T(8,128)(2,1)}, bf16[256,32]{1,0:T(8,128)(2,1)S(1)}, u32[]{:S(2)}, u32[]{:S(2)}) collective-permute-start(bf16[256,32]{1,0:T(8,128)(2,1)} %get-tuple-element.11), channel_id=1, source_target_pairs={{16,0},{32,16},{48,32},{64,48},{80,64},{96,80},{112,96},{128,112},... | collective-permute-start | bytes 49160 | tf_op jit(solution)/shard_map/ppermute | solution.py:27
  21.9 70.4 %collective-permute-start = (bf16[256,32]{1,0:T(8,128)(2,1)}, bf16[256,32]{1,0:T(8,128)(2,1)}, u32[]{:S(2)}, u32[]{:S(2)}) collective-permute-start(bf16[256,32]{1,0:T(8,128)(2,1)} %get-tuple-element.12), channel_id=1, source_target_pairs={{0,16},{16,32},{32,48},{48,64},{64,80},{80,96},{96,112},{112,128},... | collective-permute-start | bytes 49160 | tf_op jit(solution)/shard_map/ppermute | solution.py:26
  64.9 7.8 %collective-permute-start.3 = (bf16[2,256,32]{1,2,0:T(8,128)(2,1)}, bf16[2,256,32]{1,2,0:T(8,128)(2,1)S(1)}, u32[]{:S(2)}, u32[]{:S(2)}) collective-permute-start(bf16[2,256,32]{1,2,0:T(8,128)(2,1)} %collective-permute-done.2), channel_id=1, source_target_pairs={{0,2},{1,3},{2,0},{3,1},{4,6},{5,7},{6,4},{7,5},{8,10},{9,11},{10,... | collective-permute-start | bytes 98312 | tf_op jit(solution)/shard_map/ppermute | solution.py:16
  72.8 11.2 %collective-permute-start.4 = (bf16[2,256,32]{1,2,0:T(8,128)(2,1)S(1)}, bf16[2,256,32]{1,2,0:T(8,128)(2,1)}, u32[]{:S(2)}, u32[]{:S(2)}) collective-permute-start(bf16[2,256,32]{1,2,0:T(8,128)(2,1)S(1)} %collective-permute-done.3), channel_id=1, source_target_pairs={{0,4},{1,5},{2,6},{3,7},{4,0},{5,1},{6,2},{7,3},{8,12},{9,13},{10,... | collective-permute-start | bytes 98312 | tf_op jit(solution)/shard_map/ppermute | solution.py:16
  84.0 15.6 %collective-permute-start.5 = (bf16[2,256,32]{1,2,0:T(8,128)(2,1)}, bf16[2,256,32]{1,2,0:T(8,128)(2,1)S(1)}, u32[]{:S(2)}, u32[]{:S(2)}) collective-permute-start(bf16[2,256,32]{1,2,0:T(8,128)(2,1)} %collective-permute-done.4), channel_id=1, source_target_pairs={{0,8},{1,9},{2,10},{3,11},{4,12},{5,13},{6,14},{7,15},{8,0},{9,1},... | collective-permute-start | bytes 98312 | tf_op jit(solution)/shard_map/ppermute | solution.py:16
  103.4 20.3 %copy-start.4 = (f32[256]{0:T(256)S(1)}, f32[256]{0:T(256)}, u32[]{:S(2)}) copy-start(f32[256]{0:T(256)} %param.7) | copy-start | bytes 3076
Sparse Core Ops, SparseCore 0:
  9.4 114.1 all-gather.1
where the time goes:
time: 139 us
  blocking collectives  36.6 us (26%)
  waiting for transfers between devices  30.8 us (22%)
  starting transfers between devices  24 us (17%)
  between operations  16.6 us (12%)
  local copies, waits for them, and re-layouts  16.4 us (12%)
  matrix products  8.43 us (6%)
  other arithmetic  6.14 us (4%)
    psum x1, blocking collectives, per_device(): flux = lax.psum(partial_flux, 'vel')  36.6 us
    ppermute x4, starting transfers between devices, swapped(): lax.ppermute(value, axis, [(i, i ^ 1 << distance) for i in range(lax.axis...  18 us
    all_gather x1, waiting for transfers between devices, per_device(): shard_piece = lax.all_gather(lowered, 'vel', axis=0, tiled=True)  16.7 us
    ppermute x4, waiting for transfers between devices, swapped(): lax.ppermute(value, axis, [(i, i ^ 1 << distance) for i in range(lax.axis...  14.1 us
    dot_general x1, matrix products, per_device(): running = jnp.dot(kernel, shard_piece, preferred_element_type=jnp.float32)  8.43 us
    ppermute x1, starting transfers between devices, extended(): after = lax.ppermute(initial, axis, down)  4.04 us
    slice x2, local copies, waits for them, and re-layouts, per_device(): walls = jnp.stack([lowered[:, 0::NY], lowered[:, NY - 1::NY]])  3.37 us
  transfers between devices with their start and end apart: 7, of which 4 were waited for; matrix products, arithmetic and copies ran while one was open for 15% of the time, Pallas kernels for 0%

commit v1 on v0

v1 whole, which is shorter than its diff:
```python
import functools

import jax
import jax.numpy as jnp
import numpy as np
from jax import lax
from jax.experimental import pallas as pl
from jax.experimental.pallas import tpu as pltpu
from jax.sharding import PartitionSpec as P

NV1 = 16
NY = 32
NCLASS = 8
SPACING = 9.6 / NV1
MIDDLE = (NV1 - 1) / 2.0
EXTRA = 16
ADD_AT = 4
CHAINS = (0, 2, 1)

courant_x = 0.05
courant_y = 0.15


POINTS = (np.arange(NV1) - MIDDLE) * SPACING
WEIGHTS = np.exp(-0.5 * POINTS * POINTS)
ZSUM = float(WEIGHTS.sum())
OUTFLOW = float((POINTS * WEIGHTS)[POINTS > 0].sum() / ZSUM)


def base_kernel(scal_ref, d_ref, halo_ref, head_ref, tail_ref, freq_ref, out_ref):
    rows, cells = d_ref.shape
    speed = scal_ref[0]
    upward = scal_ref[1]
    core = scal_ref[2]
    y_place = lax.broadcasted_iota(jnp.int32, (NV1, cells), 1) % NY
    lane = lax.broadcasted_iota(jnp.int32, (NV1, 128), 1)

    def halves(y_shift, y_edge):
        def chunk(positive, i, carry):
            here = pl.ds(pl.multiple_of(i * NV1, NV1), NV1)
            speed_x = courant_x * jnp.abs((i.astype(jnp.float32) - MIDDLE) * SPACING)
            g = d_ref[here, :]
            halo = halo_ref[here, :].astype(jnp.float32)
            if positive:
                outside = jnp.where(core == 0.0, halo, tail_ref[here, :].astype(jnp.float32))
                beside = pltpu.roll(g, NY, 1)
                tile = jnp.where(lane < NY, pltpu.roll(outside, NY, 1), beside[:, :128])
                beside = jnp.concatenate([tile, beside[:, 128:]], axis=1)
            else:
                outside = jnp.where(core == 0.0, head_ref[here, :].astype(jnp.float32), halo)
                beside = pltpu.roll(g, cells - NY, 1)
                tile = jnp.where(lane >= 128 - NY, pltpu.roll(outside, 128 - NY, 1), beside[:, cells - 128 :])
                beside = jnp.concatenate([beside[:, : cells - 128], tile], axis=1)
            over = jnp.where(y_place == y_edge, 0.0, pltpu.roll(g, y_shift, 1))
            out_ref[here, :] = g - (speed_x * (g - beside) + speed * (g - over)) - freq_ref[here, :] * g
            return carry

        lax.fori_loop(0, rows // NV1 // 2, functools.partial(chunk, False), 0)
        lax.fori_loop(rows // NV1 // 2, rows // NV1, functools.partial(chunk, True), 0)

    @pl.when(upward > 0.0)
    def _():
        halves(1, 0)

    @pl.when(upward <= 0.0)
    def _():
        halves(cells - 1, NY - 1)


def base_part(scal, distribution, halo, near, far, frequency):
    rows, cells = distribution.shape
    smem = pl.BlockSpec(memory_space=pltpu.SMEM)
    whole = pl.BlockSpec((rows, cells), lambda i: (0, 0))
    thin = pl.BlockSpec((rows, 128), lambda i: (0, 0))
    last = far.shape[1] // 128 - 1
    return pl.pallas_call(
        base_kernel,
        grid=(1,),
        out_shape=jax.ShapeDtypeStruct(distribution.shape, jnp.float32),
        in_specs=[smem, whole, thin, thin, pl.BlockSpec((rows, 128), lambda i: (0, last)), pl.BlockSpec((rows, 1), lambda i: (0, 0))],
        out_specs=whole,
        cost_estimate=pl.CostEstimate(flops=10_000_000, bytes_accessed=3_000_000, transcendentals=0),
    )(scal, distribution, halo, near, far, frequency)


def split_kernel(core_ref, d_ref, first_ref, last_ref, near_ref, far_ref, edge_ref):
    cells = d_ref.shape[1]
    low = d_ref[...].astype(jnp.bfloat16)
    first_ref[...] = low[:, : first_ref.shape[1]]
    last_ref[...] = low[:, first_ref.shape[1] :]
    near_ref[...] = low[:, : near_ref.shape[1]]
    far_ref[...] = low[:, near_ref.shape[1] :]

    @pl.when(core_ref[0] == 0)
    def _():
        edge_ref[...] = low[:, :128]

    @pl.when(core_ref[0] != 0)
    def _():
        edge_ref[...] = low[:, cells - 128 :]


def split_part(core, distribution, cut, mixed):
    rows, cells = distribution.shape
    widths = (cut, cells - cut, mixed, cells - mixed, 128)
    part = rows // 4
    return pl.pallas_call(
        split_kernel,
        grid=(4,),
        out_shape=[jax.ShapeDtypeStruct((rows, width), jnp.bfloat16) for width in widths],
        in_specs=[pl.BlockSpec(memory_space=pltpu.SMEM), pl.BlockSpec((part, cells), lambda i: (i, 0))],
        out_specs=[pl.BlockSpec((part, width), lambda i: (i, 0)) for width in widths],
        cost_estimate=pl.CostEstimate(flops=1_000_000, bytes_accessed=3_000_000, transcendentals=0),
    )(core, distribution)


def per_device(distribution, kernel, frequency, accommodation, wall_class):
    rows, cells = distribution.shape
    ranks = lax.axis_size("vel")
    places = lax.axis_size("space")
    rank = lax.axis_index("vel")
    core = lax.axis_index("space") & 1
    f32, bf16 = jnp.float32, jnp.bfloat16
    half = ranks // 2

    ring = [(s * ranks + v, s * ranks + (v + (1 if s % 2 == 0 else -1)) % ranks) for s in range(places) for v in range(ranks)]
    pair = [(s, s ^ 1) for s in range(places)]
    beyond = [(s, (s + (1 if s % 2 else -1)) % places) for s in range(places)]

    def hop(values):
        return lax.ppermute(values, ("space", "vel"), ring)

    def swap(values):
        return lax.ppermute(values, "space", pair)

    cut, mixed = 5 * cells // 8, cells // 4
    own = cells - cut
    first, last, near, far, edge = split_part(core[None], distribution, cut, mixed)
    far = swap(far)
    near = swap(near)
    held = [first, jnp.concatenate([last, near], axis=1), far]

    lower_half = rank < half
    at_wall = lax.broadcasted_iota(jnp.int32, (1, cells), 1) % NY == jnp.where(lower_half, NY - 1, 0)
    classes = jnp.where(lower_half, wall_class[1], wall_class[0])
    class_ids = lax.iota(jnp.int32, NCLASS)
    alpha = jnp.sum(jnp.where(classes[:, None] == class_ids[None, :], accommodation[None, :], 0.0), axis=1)
    alpha = jnp.repeat(alpha, NY)[None, :]
    vel_y = (rank.astype(f32) - MIDDLE) * SPACING
    speed = courant_y * jnp.abs(vel_y)
    keep = jnp.where(at_wall, speed * (1.0 - alpha), 0.0)
    share = jnp.where(at_wall, alpha * (0.5 * SPACING / OUTFLOW), 0.0)
    their_keep = swap(keep)
    keeps = [keep[:, :cut], jnp.concatenate([keep[:, cut:], their_keep[:, :mixed]], axis=1), their_keep[:, mixed:]]

    block = lax.broadcasted_iota(jnp.int32, (EXTRA, kernel.shape[1]), 1) // rows
    outgoing = (block < half) != lower_half
    weight = jnp.where(outgoing, jnp.abs(2 * block - (NV1 - 1)), 0).astype(bf16)
    wide = jnp.concatenate([kernel, weight], axis=0)

    def origin(step):
        return (rank + jnp.where(core == 0, -step, step)) & (ranks - 1)

    def part(step, values):
        return jnp.dot(
            lax.dynamic_slice_in_dim(wide, origin(step) * rows, rows, axis=1), values, preferred_element_type=f32
        )

    halo = lax.ppermute(edge, "space", beyond)
    scal = jnp.stack([speed, jnp.where(vel_y > 0.0, 1.0, -1.0), core.astype(f32)])
    base = base_part(scal, distribution, halo, near, far, frequency[:, None])

    sums = [part(0, first), jnp.pad(part(0, last), ((0, 0), (0, mixed))), None]
    for step in range(1, half):
        for j in CHAINS:
            held[j] = hop(held[j])
            if step == ADD_AT and j == 0:
                held[0], sums[0], base = lax.optimization_barrier((held[0], sums[0], base))
            elif step > 1 and step < half - 1:
                held[j], sums[j] = lax.optimization_barrier((held[j], sums[j]))
        for j in CHAINS:
            mirrored = jnp.where(origin(step) == ranks - 1 - rank, keeps[j], 0.0)
            given = part(step, held[j])
            if step % 2 == 1:
                given = given + jnp.pad(mirrored * held[j].astype(f32), ((0, EXTRA), (0, 0)))
            if step == ADD_AT and j == 0:
                given = given + jnp.pad(base[:, :cut], ((0, EXTRA), (0, 0)))
            if step == ADD_AT and j == 1:
                given = given + jnp.pad(base[:, cut:], ((0, EXTRA), (0, mixed)))
            sums[j] = given if sums[j] is None else sums[j] + given
    final = jnp.concatenate([hop(held[0]), hop(held[1][:, :own])], axis=1)
    given = swap(jnp.concatenate([sums[1][:, own:], sums[2]], axis=1))

    index = lax.iota(jnp.int32, rows)
    vel_x = ((index // NV1 % NV1).astype(f32) - MIDDLE) * SPACING
    vel_z = ((index % NV1).astype(f32) - MIDDLE) * SPACING
    maxwell = jnp.exp(-0.5 * (vel_x * vel_x + vel_y * vel_y + vel_z * vel_z)) * (speed / ZSUM**3)

    mine = jnp.concatenate([sums[0], sums[1][:, :own]], axis=1)
    total = mine + given + part(half, final)
    return total[:rows] + maxwell[:, None] * (total[rows : rows + 1] * share)


def solution(mesh):
    placed = (P("vel", "space"), P("vel", None), P("vel"), P(), P(None, "space"))
    return jax.shard_map(per_device, mesh=mesh, in_specs=placed, out_specs=P("vel", "space"), check_vma=False)
```

time: 139 us -> 169 us (1.22)
  the two profiles are of different devices: /device:TPU:2 before, /device:TPU:6 now
where the time goes in v1:
time: 169 us; the launch traced here: 167 us
  starting transfers between devices  80.8 us (48%)
  waiting for transfers between devices  45.1 us (27%)
  other arithmetic  15.7 us (9%)
  matrix products  12.4 us (7%)
  Pallas kernels  7.5 us (4%)
  local copies, waits for them, and re-layouts  5 us (3%)
    ppermute x23, starting transfers between devices, hop(): return lax.ppermute(values, ('space', 'vel'), ring)  60.7 us
    ppermute x23, waiting for transfers between devices, hop(): return lax.ppermute(values, ('space', 'vel'), ring)  45.1 us
    ppermute x4, starting transfers between devices, swap(): return lax.ppermute(values, 'space', pair)  14.8 us
    dot_general x24, matrix products, part(): jnp.dot(lax.dynamic_slice_in_dim(wide, origin(step) * rows, rows, axis=1)...  12.4 us
    ppermute x1, starting transfers between devices, per_device(): halo = lax.ppermute(edge, 'space', beyond)  5.29 us
    pallas_call x1, Pallas kernels, base_part(): pl.pallas_call(base_kernel, grid=(1,), out_shape=jax.ShapeDtypeStruct(dis...  4.13 us
    select_n x3, other arithmetic, per_device(): mirrored = jnp.where(origin(step) == ranks - 1 - rank, keeps[j], 0.0)  3.86 us
  transfers between devices with their start and end apart: 28, of which 12 were waited for; matrix products, arithmetic and copies ran while one was open for 18% of the time, Pallas kernels for 2%

profile of v1, /device:TPU:6, one launch (start us, length us, event | category | flops | bytes accessed | tf_op | source)
XLA Modules:
  0.0 167.3 jit_solution(9197056140105591775)
XLA Ops:
  0.0 3.4 %shard_map.55 = (bf16[256,640]{1,0:T(8,128)(2,1)}, bf16[256,384]{1,0:T(8,128)(2,1)}, bf16[256,256]{1,0:T(8,128)(2,1)}, bf16[256,768]{1,0:T(8,128)(2,1)}, bf16[256,128]{1,0:T(8,128)(2,1)}) custom-call(s32[1]{0:T(128)} %bitcast.core_ref, f32[256,1024]{1,0:T(8,128)} %d_ref.3), custom_call_target="tpu_custom_call" | custom-call | flops 1000000 | bytes 3000000 | tf_op jit(solution)/shard_map/pallas_call | solution.py:107
  3.4 3.8 %collective-permute-start = (bf16[256,640]{1,0:T(8,128)(2,1)}, bf16[256,640]{1,0:T(8,128)(2,1)S(1)}, u32[]{:S(2)}, u32[]{:S(2)}) collective-permute-start(bf16[256,640]{1,0:T(8,128)(2,1)} %get-tuple-element.41), channel_id=1, source_target_pairs={{0,1},{1,2},{2,3},{3,4},{4,5},{5,6},{6,7},{7,8},{8,9},{9,10},{10,1... | collective-permute-start | bytes 983048 | tf_op jit(solution)/shard_map/ppermute | solution.py:131
  7.2 9.0 %collective-permute-start.6 = (bf16[256,768]{1,0:T(8,128)(2,1)}, bf16[256,768]{1,0:T(8,128)(2,1)}, u32[]{:S(2)}, u32[]{:S(2)}) collective-permute-start(bf16[256,768]{1,0:T(8,128)(2,1)} %get-tuple-element.48), channel_id=1, source_target_pairs={{0,16},{16,0},{32,48},{48,32},{64,80},{80,64},{96,112},{112,96},{1... | collective-permute-start | bytes 1179656 | tf_op jit(solution)/shard_map/ppermute | solution.py:134
  16.2 1.9 %collective-permute-start.5 = (bf16[256,256]{1,0:T(8,128)(2,1)}, bf16[256,256]{1,0:T(8,128)(2,1)}, u32[]{:S(2)}, u32[]{:S(2)}) collective-permute-start(bf16[256,256]{1,0:T(8,128)(2,1)} %get-tuple-element.47), channel_id=1, source_target_pairs={{0,16},{16,0},{32,48},{48,32},{64,80},{80,64},{96,112},{112,96},{1... | collective-permute-start | bytes 393224 | tf_op jit(solution)/shard_map/ppermute | solution.py:134
  18.2 5.3 %collective-permute-start.4 = (bf16[256,128]{1,0:T(8,128)(2,1)}, bf16[256,128]{1,0:T(8,128)(2,1)}, u32[]{:S(2)}, u32[]{:S(2)}) collective-permute-start(bf16[256,128]{1,0:T(8,128)(2,1)} %get-tuple-element.46), channel_id=1, source_target_pairs={{0,496},{16,32},{32,16},{48,64},{64,48},{80,96},{96,80},{112,128},... | collective-permute-start | bytes 196616 | tf_op jit(solution)/shard_map/ppermute | solution.py:169
  26.2 1.9 %collective-permute-start.12 = (f32[1,1024]{1,0:T(1,128)}, f32[1,1024]{1,0:T(1,128)}, u32[]{:S(2)}, u32[]{:S(2)}) collective-permute-start(f32[1,1024]{1,0:T(1,128)} %compare_select_fusion.1), channel_id=1, source_target_pairs={{0,16},{16,0},{32,48},{48,32},{64,80},{80,64},{96,112},{112,96},{1... | collective-permute-start | bytes 12296 | tf_op jit(solution)/shard_map/ppermute | solution.py:134
  31.6 2.0 %fusion.74 = f32[272,384]{1,0:T(8,128)} fusion(bf16[272,256]{1,0:T(8,128)(2,1)} %copy-done.3, bf16[256,384]{1,0:T(8,128)(2,1)} %get-tuple-element.56), kind=kOutput, calls=%fused_computation.143 | convolution fusion | flops 53477376 | bytes 753664 | tf_op jit(solution)/shard_map/dot_general | solution.py:165
  42.8 1.9 %collective-permute-start.10 = (bf16[256,640]{1,0:T(8,128)(2,1)}, bf16[256,640]{1,0:T(8,128)(2,1)}, u32[]{:S(2)}, u32[]{:S(2)}) collective-permute-start(bf16[256,640]{1,0:T(8,128)(2,1)} %pad_maximum_fusion.1), channel_id=1, source_target_pairs={{0,1},{1,2},{2,3},{3,4},{4,5},{5,6},{6,7},{7,8},{8,9},{9,10},{10,1... | collective-permute-start | bytes 983048 | tf_op jit(solution)/shard_map/ppermute | solution.py:131
  44.7 1.9 %collective-permute-start.1 = (bf16[256,640]{1,0:T(8,128)(2,1)S(1)}, bf16[256,640]{1,0:T(8,128)(2,1)}, u32[]{:S(2)}, u32[]{:S(2)}) collective-permute-start(bf16[256,640]{1,0:T(8,128)(2,1)S(1)} %collective-permute-done), channel_id=1, source_target_pairs={{0,1},{1,2},{2,3},{3,4},{4,5},{5,6},{6,7},{7,8},{8,9},{9,10},{10,1... | collective-permute-start | bytes 983048 | tf_op jit(solution)/shard_map/ppermute | solution.py:131
  48.5 2.0 %collective-permute-start.18 = (bf16[256,768]{1,0:T(8,128)(2,1)}, bf16[256,768]{1,0:T(8,128)(2,1)}, u32[]{:S(2)}, u32[]{:S(2)}) collective-permute-start(bf16[256,768]{1,0:T(8,128)(2,1)} %collective-permute-done.6.tail_ref), channel_id=1, source_target_pairs={{0,1},{1,2},{2,3},{3,4},{4,5},{5,6},{6,7},{7,8},{8,9},{9,10},{10,1... | collective-permute-start | bytes 1179656 | tf_op jit(solution)/shard_map/ppermute | solution.py:131
  50.6 4.1 %shard_map.56 = f32[256,1024]{1,0:T(8,128)} custom-call(f32[3]{0:T(128)} %pad_maximum_fusion.3.scal_ref, f32[256,1024]{1,0:T(8,128)} %d_ref.3, bf16[256,128]{1,0:T(8,128)(2,1)} %collective-permute-done.4.halo_ref, bf16[256,256]{1,0:T(8,128)(2,1)} %collective-permute-done.5.head_ref, bf16[256,768]{1,0:T(8,128)(2,1)} %collective-permute-done.6.tail_ref, ...), custom_call_target="tpu_custom_call" | custom-call | flops 10000000 | bytes 3000000 | tf_op jit(solution)/shard_map/pallas_call | solution.py:76
  54.7 3.6 %collective-permute-start.11 = (bf16[256,640]{1,0:T(8,128)(2,1)}, bf16[256,640]{1,0:T(8,128)(2,1)S(1)}, u32[]{:S(2)}, u32[]{:S(2)}) collective-permute-start(bf16[256,640]{1,0:T(8,128)(2,1)} %collective-permute-done.10), channel_id=1, source_target_pairs={{0,1},{1,2},{2,3},{3,4},{4,5},{5,6},{6,7},{7,8},{8,9},{9,10},{10,1... | collective-permute-start | bytes 983048 | tf_op jit(solution)/shard_map/ppermute | solution.py:131
  60.8 3.8 %collective-permute-start.2 = (bf16[256,640]{1,0:T(8,128)(2,1)}, bf16[256,640]{1,0:T(8,128)(2,1)S(1)}, u32[]{:S(2)}, u32[]{:S(2)}) collective-permute-start(bf16[256,640]{1,0:T(8,128)(2,1)} %collective-permute-done.1), channel_id=1, source_target_pairs={{0,1},{1,2},{2,3},{3,4},{4,5},{5,6},{6,7},{7,8},{8,9},{9,10},{10,1... | collective-permute-start | bytes 983048 | tf_op jit(solution)/shard_map/ppermute | solution.py:131
  66.0 3.8 %collective-permute-start.13 = (bf16[256,640]{1,0:T(8,128)(2,1)S(1)}, bf16[256,640]{1,0:T(8,128)(2,1)S(1)}, u32[]{:S(2)}, u32[]{:S(2)}) collective-permute-start(bf16[256,640]{1,0:T(8,128)(2,1)S(1)} %collective-permute-done.11), channel_id=1, source_target_pairs={{0,1},{1,2},{2,3},{3,4},{4,5},{5,6},{6,7},{7,8},{8,9},{9,10},{10,1... | collective-permute-start | bytes 983048 | tf_op jit(solution)/shard_map/ppermute | solution.py:131
  70.2 5.0 %collective-permute-start.19 = (bf16[256,768]{1,0:T(8,128)(2,1)}, bf16[256,768]{1,0:T(8,128)(2,1)S(1)}, u32[]{:S(2)}, u32[]{:S(2)}) collective-permute-start(bf16[256,768]{1,0:T(8,128)(2,1)} %collective-permute-done.18), channel_id=1, source_target_pairs={{0,1},{1,2},{2,3},{3,4},{4,5},{5,6},{6,7},{7,8},{8,9},{9,10},{10,1... | collective-permute-start | bytes 1179656 | tf_op jit(solution)/shard_map/ppermute | solution.py:131
  77.6 2.9 %collective-permute-start.3 = (bf16[256,640]{1,0:T(8,128)(2,1)S(1)}, bf16[256,640]{1,0:T(8,128)(2,1)S(1)}, u32[]{:S(2)}, u32[]{:S(2)}) collective-permute-start(bf16[256,640]{1,0:T(8,128)(2,1)S(1)} %collective-permute-done.2), channel_id=1, source_target_pairs={{0,1},{1,2},{2,3},{3,4},{4,5},{5,6},{6,7},{7,8},{8,9},{9,10},{10,1... | collective-permute-start | bytes 983048 | tf_op jit(solution)/shard_map/ppermute | solution.py:131
  81.0 3.6 %collective-permute-start.14 = (bf16[256,640]{1,0:T(8,128)(2,1)S(1)}, bf16[256,640]{1,0:T(8,128)(2,1)S(1)}, u32[]{:S(2)}, u32[]{:S(2)}) collective-permute-start(bf16[256,640]{1,0:T(8,128)(2,1)S(1)} %collective-permute-done.13), channel_id=1, source_target_pairs={{0,1},{1,2},{2,3},{3,4},{4,5},{5,6},{6,7},{7,8},{8,9},{9,10},{10,1... | collective-permute-start | bytes 983048 | tf_op jit(solution)/shard_map/ppermute | solution.py:131
  85.4 2.3 %collective-permute-start.20 = (bf16[256,768]{1,0:T(8,128)(2,1)S(1)}, bf16[256,768]{1,0:T(8,128)(2,1)S(1)}, u32[]{:S(2)}, u32[]{:S(2)}) collective-permute-start(bf16[256,768]{1,0:T(8,128)(2,1)S(1)} %collective-permute-done.19), channel_id=1, source_target_pairs={{0,1},{1,2},{2,3},{3,4},{4,5},{5,6},{6,7},{7,8},{8,9},{9,10},{10,1... | collective-permute-start | bytes 1179656 | tf_op jit(solution)/shard_map/ppermute | solution.py:131
  87.9 3.1 %collective-permute-start.7 = (bf16[256,640]{1,0:T(8,128)(2,1)S(1)}, bf16[256,640]{1,0:T(8,128)(2,1)S(1)}, u32[]{:S(2)}, u32[]{:S(2)}) collective-permute-start(bf16[256,640]{1,0:T(8,128)(2,1)S(1)} %collective-permute-done.3), channel_id=1, source_target_pairs={{0,1},{1,2},{2,3},{3,4},{4,5},{5,6},{6,7},{7,8},{8,9},{9,10},{10,1... | collective-permute-start | bytes 983048 | tf_op jit(solution)/shard_map/ppermute | solution.py:131
  91.3 3.7 %collective-permute-start.15 = (bf16[256,640]{1,0:T(8,128)(2,1)S(1)}, bf16[256,640]{1,0:T(8,128)(2,1)S(1)}, u32[]{:S(2)}, u32[]{:S(2)}) collective-permute-start(bf16[256,640]{1,0:T(8,128)(2,1)S(1)} %collective-permute-done.14), channel_id=1, source_target_pairs={{0,1},{1,2},{2,3},{3,4},{4,5},{5,6},{6,7},{7,8},{8,9},{9,10},{10,1... | collective-permute-start | bytes 983048 | tf_op jit(solution)/shard_map/ppermute | solution.py:131
  96.4 1.9 %collective-permute-start.21 = (bf16[256,768]{1,0:T(8,128)(2,1)S(1)}, bf16[256,768]{1,0:T(8,128)(2,1)S(1)}, u32[]{:S(2)}, u32[]{:S(2)}) collective-permute-start(bf16[256,768]{1,0:T(8,128)(2,1)S(1)} %collective-permute-done.20), channel_id=1, source_target_pairs={{0,1},{1,2},{2,3},{3,4},{4,5},{5,6},{6,7},{7,8},{8,9},{9,10},{10,1... | collective-permute-start | bytes 1179656 | tf_op jit(solution)/shard_map/ppermute | solution.py:131
  109.9 4.7 %collective-permute-done.16 = bf16[256,640]{1,0:T(8,128)(2,1)S(1)} collective-permute-done((bf16[256,640]{1,0:T(8,128)(2,1)S(1)}, bf16[256,640]{1,0:T(8,128)(2,1)S(1)}, u32[]{:S(2)}, u32[]{:S(2)}) %collective-permute-start.16) | collective-permute-done | bytes 327712 | tf_op jit(solution)/shard_map/ppermute | solution.py:131
  116.8 2.0 %collective-permute-done.22 = bf16[256,768]{1,0:T(8,128)(2,1)S(1)} collective-permute-done((bf16[256,768]{1,0:T(8,128)(2,1)S(1)}, bf16[256,768]{1,0:T(8,128)(2,1)S(1)}, u32[]{:S(2)}, u32[]{:S(2)}) %collective-permute-start.22) | collective-permute-done | bytes 393248 | tf_op jit(solution)/shard_map/ppermute | solution.py:131
  121.2 3.6 %collective-permute-done.17 = bf16[256,640]{1,0:T(8,128)(2,1)S(1)} collective-permute-done((bf16[256,640]{1,0:T(8,128)(2,1)S(1)}, bf16[256,640]{1,0:T(8,128)(2,1)S(1)}, u32[]{:S(2)}, u32[]{:S(2)}) %collective-permute-start.17) | collective-permute-done | bytes 327712 | tf_op jit(solution)/shard_map/ppermute | solution.py:131
  124.9 4.9 %collective-permute-done.23 = bf16[256,768]{1,0:T(8,128)(2,1)S(1)} collective-permute-done((bf16[256,768]{1,0:T(8,128)(2,1)S(1)}, bf16[256,768]{1,0:T(8,128)(2,1)S(1)}, u32[]{:S(2)}, u32[]{:S(2)}) %collective-permute-start.23) | collective-permute-done | bytes 393248 | tf_op jit(solution)/shard_map/ppermute | solution.py:131
  132.3 8.3 %collective-permute-done.24 = bf16[256,768]{1,0:T(8,128)(2,1)S(1)} collective-permute-done((bf16[256,768]{1,0:T(8,128)(2,1)S(1)}, bf16[256,768]{1,0:T(8,128)(2,1)S(1)}, u32[]{:S(2)}, u32[]{:S(2)}) %collective-permute-start.24) | collective-permute-done | bytes 393248 | tf_op jit(solution)/shard_map/ppermute | solution.py:131
  141.1 1.9 %collective-permute-start.25 = (f32[272,1024]{1,0:T(8,128)S(1)}, f32[272,1024]{1,0:T(8,128)S(1)}, u32[]{:S(2)}, u32[]{:S(2)}) collective-permute-start(f32[272,1024]{1,0:T(8,128)S(1)} %pad_maximum_fusion), channel_id=1, source_target_pairs={{0,16},{16,0},{32,48},{48,32},{64,80},{80,64},{96,112},{112,96},{1... | collective-permute-start | bytes 3342344 | tf_op jit(solution)/shard_map/ppermute | solution.py:134
  143.4 1.9 %collective-permute-start.9 = (bf16[256,640]{1,0:T(8,128)(2,1)S(1)}, bf16[256,640]{1,0:T(8,128)(2,1)S(1)}, u32[]{:S(2)}, u32[]{:S(2)}) collective-permute-start(bf16[256,640]{1,0:T(8,128)(2,1)S(1)} %collective-permute-done.8), channel_id=1, source_target_pairs={{0,1},{1,2},{2,3},{3,4},{4,5},{5,6},{6,7},{7,8},{8,9},{9,10},{10,1... | collective-permute-start | bytes 983048 | tf_op jit(solution)/shard_map/ppermute | solution.py:131
  145.6 8.0 %collective-permute-done.9 = bf16[256,640]{1,0:T(8,128)(2,1)S(1)} collective-permute-done((bf16[256,640]{1,0:T(8,128)(2,1)S(1)}, bf16[256,640]{1,0:T(8,128)(2,1)S(1)}, u32[]{:S(2)}, u32[]{:S(2)}) %collective-permute-start.9) | collective-permute-done | bytes 327712 | tf_op jit(solution)/shard_map/ppermute | solution.py:131
  155.6 1.9 %collective-permute-start.27 = (bf16[256,384]{1,0:T(8,128)(2,1)S(1)}, bf16[256,384]{1,0:T(8,128)(2,1)S(1)}, u32[]{:S(2)}, u32[]{:S(2)}) collective-permute-start(bf16[256,384]{1,0:T(8,128)(2,1)S(1)} %slice.58), channel_id=1, source_target_pairs={{0,1},{1,2},{2,3},{3,4},{4,5},{5,6},{6,7},{7,8},{8,9},{9,10},{10,1... | collective-permute-start | bytes 589832 | tf_op jit(solution)/shard_map/ppermute | solution.py:131
  157.9 5.9 %collective-permute-done.26 = bf16[256,640]{1,0:T(8,128)(2,1)S(1)} collective-permute-done((bf16[256,640]{1,0:T(8,128)(2,1)S(1)}, bf16[256,640]{1,0:T(8,128)(2,1)S(1)}, u32[]{:S(2)}, u32[]{:S(2)}) %collective-permute-start.26) | collective-permute-done | bytes 327712 | tf_op jit(solution)/shard_map/ppermute | solution.py:131
  163.8 2.1 %collective-permute-done.27 = bf16[256,384]{1,0:T(8,128)(2,1)S(1)} collective-permute-done((bf16[256,384]{1,0:T(8,128)(2,1)S(1)}, bf16[256,384]{1,0:T(8,128)(2,1)S(1)}, u32[]{:S(2)}, u32[]{:S(2)}) %collective-permute-start.27) | collective-permute-done | bytes 196640 | tf_op jit(solution)/shard_map/ppermute | solution.py:131
  (129 shorter events, 50.0 us)
Async XLA Ops:
  3.4 41.3 %collective-permute-start = (bf16[256,640]{1,0:T(8,128)(2,1)}, bf16[256,640]{1,0:T(8,128)(2,1)S(1)}, u32[]{:S(2)}, u32[]{:S(2)}) collective-permute-start(bf16[256,640]{1,0:T(8,128)(2,1)} %get-tuple-element.41), channel_id=1, source_target_pairs={{0,1},{1,2},{2,3},{3,4},{4,5},{5,6},{6,7},{7,8},{8,9},{9,10},{10,1... | collective-permute-start | bytes 983048 | tf_op jit(solution)/shard_map/ppermute | solution.py:131
  7.2 41.3 %collective-permute-start.6 = (bf16[256,768]{1,0:T(8,128)(2,1)}, bf16[256,768]{1,0:T(8,128)(2,1)}, u32[]{:S(2)}, u32[]{:S(2)}) collective-permute-start(bf16[256,768]{1,0:T(8,128)(2,1)} %get-tuple-element.48), channel_id=1, source_target_pairs={{0,16},{16,0},{32,48},{48,32},{64,80},{80,64},{96,112},{112,96},{1... | collective-permute-start | bytes 1179656 | tf_op jit(solution)/shard_map/ppermute | solution.py:134
  16.2 24.8 %collective-permute-start.5 = (bf16[256,256]{1,0:T(8,128)(2,1)}, bf16[256,256]{1,0:T(8,128)(2,1)}, u32[]{:S(2)}, u32[]{:S(2)}) collective-permute-start(bf16[256,256]{1,0:T(8,128)(2,1)} %get-tuple-element.47), channel_id=1, source_target_pairs={{0,16},{16,0},{32,48},{48,32},{64,80},{80,64},{96,112},{112,96},{1... | collective-permute-start | bytes 393224 | tf_op jit(solution)/shard_map/ppermute | solution.py:134
  18.2 32.4 %collective-permute-start.4 = (bf16[256,128]{1,0:T(8,128)(2,1)}, bf16[256,128]{1,0:T(8,128)(2,1)}, u32[]{:S(2)}, u32[]{:S(2)}) collective-permute-start(bf16[256,128]{1,0:T(8,128)(2,1)} %get-tuple-element.46), channel_id=1, source_target_pairs={{0,496},{16,32},{32,16},{48,64},{64,48},{80,96},{96,80},{112,128},... | collective-permute-start | bytes 196616 | tf_op jit(solution)/shard_map/ppermute | solution.py:169
  26.2 11.5 %collective-permute-start.12 = (f32[1,1024]{1,0:T(1,128)}, f32[1,1024]{1,0:T(1,128)}, u32[]{:S(2)}, u32[]{:S(2)}) collective-permute-start(f32[1,1024]{1,0:T(1,128)} %compare_select_fusion.1), channel_id=1, source_target_pairs={{0,16},{16,0},{32,48},{48,32},{64,80},{80,64},{96,112},{112,96},{1... | collective-permute-start | bytes 12296 | tf_op jit(solution)/shard_map/ppermute | solution.py:134
  30.7 16.7 %copy-start = (bf16[256,4096]{1,0:T(8,128)(2,1)S(1)}, bf16[256,4096]{1,0:T(8,128)(2,1)}, u32[]{:S(2)}) copy-start(bf16[256,4096]{1,0:T(8,128)(2,1)} %param.6) | copy-start | bytes 6291460
  42.8 12.0 %collective-permute-start.10 = (bf16[256,640]{1,0:T(8,128)(2,1)}, bf16[256,640]{1,0:T(8,128)(2,1)}, u32[]{:S(2)}, u32[]{:S(2)}) collective-permute-start(bf16[256,640]{1,0:T(8,128)(2,1)} %pad_maximum_fusion.1), channel_id=1, source_target_pairs={{0,1},{1,2},{2,3},{3,4},{4,5},{5,6},{6,7},{7,8},{8,9},{9,10},{10,1... | collective-permute-start | bytes 983048 | tf_op jit(solution)/shard_map/ppermute | solution.py:131
  44.7 16.1 %collective-permute-start.1 = (bf16[256,640]{1,0:T(8,128)(2,1)S(1)}, bf16[256,640]{1,0:T(8,128)(2,1)}, u32[]{:S(2)}, u32[]{:S(2)}) collective-permute-start(bf16[256,640]{1,0:T(8,128)(2,1)S(1)} %collective-permute-done), channel_id=1, source_target_pairs={{0,1},{1,2},{2,3},{3,4},{4,5},{5,6},{6,7},{7,8},{8,9},{9,10},{10,1... | collective-permute-start | bytes 983048 | tf_op jit(solution)/shard_map/ppermute | solution.py:131
  48.5 9.8 %copy-start.9 = (f32[640]{0:T(1024)S(1)}, f32[640]{0:T(1024)}, u32[]{:S(2)}) copy-start(f32[640]{0:T(1024)} %get-tuple-element.91) | copy-start | bytes 7684
  48.5 10.9 %copy-start.2 = (f32[272,384]{1,0:T(8,128)S(1)}, f32[272,384]{1,0:T(8,128)}, u32[]{:S(2)}) copy-start(f32[272,384]{1,0:T(8,128)} %fusion.74) | copy-start | bytes 1253380
  48.5 21.7 %collective-permute-start.18 = (bf16[256,768]{1,0:T(8,128)(2,1)}, bf16[256,768]{1,0:T(8,128)(2,1)}, u32[]{:S(2)}, u32[]{:S(2)}) collective-permute-start(bf16[256,768]{1,0:T(8,128)(2,1)} %collective-permute-done.6.tail_ref), channel_id=1, source_target_pairs={{0,1},{1,2},{2,3},{3,4},{4,5},{5,6},{6,7},{7,8},{8,9},{9,10},{10,1... | collective-permute-start | bytes 1179656 | tf_op jit(solution)/shard_map/ppermute | solution.py:131
  54.7 11.2 %collective-permute-start.11 = (bf16[256,640]{1,0:T(8,128)(2,1)}, bf16[256,640]{1,0:T(8,128)(2,1)S(1)}, u32[]{:S(2)}, u32[]{:S(2)}) collective-permute-start(bf16[256,640]{1,0:T(8,128)(2,1)} %collective-permute-done.10), channel_id=1, source_target_pairs={{0,1},{1,2},{2,3},{3,4},{4,5},{5,6},{6,7},{7,8},{8,9},{9,10},{10,1... | collective-permute-start | bytes 983048 | tf_op jit(solution)/shard_map/ppermute | solution.py:131
  60.8 16.8 %collective-permute-start.2 = (bf16[256,640]{1,0:T(8,128)(2,1)}, bf16[256,640]{1,0:T(8,128)(2,1)S(1)}, u32[]{:S(2)}, u32[]{:S(2)}) collective-permute-start(bf16[256,640]{1,0:T(8,128)(2,1)} %collective-permute-done.1), channel_id=1, source_target_pairs={{0,1},{1,2},{2,3},{3,4},{4,5},{5,6},{6,7},{7,8},{8,9},{9,10},{10,1... | collective-permute-start | bytes 983048 | tf_op jit(solution)/shard_map/ppermute | solution.py:131
  65.9 9.3 %copy-start.8 = (f32[768]{0:T(1024)S(1)}, f32[768]{0:T(1024)}, u32[]{:S(2)}) copy-start(f32[768]{0:T(1024)} %get-tuple-element.84) | copy-start | bytes 9220
  66.0 15.0 %collective-permute-start.13 = (bf16[256,640]{1,0:T(8,128)(2,1)S(1)}, bf16[256,640]{1,0:T(8,128)(2,1)S(1)}, u32[]{:S(2)}, u32[]{:S(2)}) collective-permute-start(bf16[256,640]{1,0:T(8,128)(2,1)S(1)} %collective-permute-done.11), channel_id=1, source_target_pairs={{0,1},{1,2},{2,3},{3,4},{4,5},{5,6},{6,7},{7,8},{8,9},{9,10},{10,1... | collective-permute-start | bytes 983048 | tf_op jit(solution)/shard_map/ppermute | solution.py:131
  70.2 14.9 %collective-permute-start.19 = (bf16[256,768]{1,0:T(8,128)(2,1)}, bf16[256,768]{1,0:T(8,128)(2,1)S(1)}, u32[]{:S(2)}, u32[]{:S(2)}) collective-permute-start(bf16[256,768]{1,0:T(8,128)(2,1)} %collective-permute-done.18), channel_id=1, source_target_pairs={{0,1},{1,2},{2,3},{3,4},{4,5},{5,6},{6,7},{7,8},{8,9},{9,10},{10,1... | collective-permute-start | bytes 1179656 | tf_op jit(solution)/shard_map/ppermute | solution.py:131
  77.6 10.2 %collective-permute-start.3 = (bf16[256,640]{1,0:T(8,128)(2,1)S(1)}, bf16[256,640]{1,0:T(8,128)(2,1)S(1)}, u32[]{:S(2)}, u32[]{:S(2)}) collective-permute-start(bf16[256,640]{1,0:T(8,128)(2,1)S(1)} %collective-permute-done.2), channel_id=1, source_target_pairs={{0,1},{1,2},{2,3},{3,4},{4,5},{5,6},{6,7},{7,8},{8,9},{9,10},{10,1... | collective-permute-start | bytes 983048 | tf_op jit(solution)/shard_map/ppermute | solution.py:131
  81.0 10.3 %collective-permute-start.14 = (bf16[256,640]{1,0:T(8,128)(2,1)S(1)}, bf16[256,640]{1,0:T(8,128)(2,1)S(1)}, u32[]{:S(2)}, u32[]{:S(2)}) collective-permute-start(bf16[256,640]{1,0:T(8,128)(2,1)S(1)} %collective-permute-done.13), channel_id=1, source_target_pairs={{0,1},{1,2},{2,3},{3,4},{4,5},{5,6},{6,7},{7,8},{8,9},{9,10},{10,1... | collective-permute-start | bytes 983048 | tf_op jit(solution)/shard_map/ppermute | solution.py:131
  85.4 11.0 %collective-permute-start.20 = (bf16[256,768]{1,0:T(8,128)(2,1)S(1)}, bf16[256,768]{1,0:T(8,128)(2,1)S(1)}, u32[]{:S(2)}, u32[]{:S(2)}) collective-permute-start(bf16[256,768]{1,0:T(8,128)(2,1)S(1)} %collective-permute-done.19), channel_id=1, source_target_pairs={{0,1},{1,2},{2,3},{3,4},{4,5},{5,6},{6,7},{7,8},{8,9},{9,10},{10,1... | collective-permute-start | bytes 1179656 | tf_op jit(solution)/shard_map/ppermute | solution.py:131
  87.9 12.1 %collective-permute-start.7 = (bf16[256,640]{1,0:T(8,128)(2,1)S(1)}, bf16[256,640]{1,0:T(8,128)(2,1)S(1)}, u32[]{:S(2)}, u32[]{:S(2)}) collective-permute-start(bf16[256,640]{1,0:T(8,128)(2,1)S(1)} %collective-permute-done.3), channel_id=1, source_target_pairs={{0,1},{1,2},{2,3},{3,4},{4,5},{5,6},{6,7},{7,8},{8,9},{9,10},{10,1... | collective-permute-start | bytes 983048 | tf_op jit(solution)/shard_map/ppermute | solution.py:131
  91.3 12.1 %collective-permute-start.15 = (bf16[256,640]{1,0:T(8,128)(2,1)S(1)}, bf16[256,640]{1,0:T(8,128)(2,1)S(1)}, u32[]{:S(2)}, u32[]{:S(2)}) collective-permute-start(bf16[256,640]{1,0:T(8,128)(2,1)S(1)} %collective-permute-done.14), channel_id=1, source_target_pairs={{0,1},{1,2},{2,3},{3,4},{4,5},{5,6},{6,7},{7,8},{8,9},{9,10},{10,1... | collective-permute-start | bytes 983048 | tf_op jit(solution)/shard_map/ppermute | solution.py:131
  96.4 11.2 %collective-permute-start.21 = (bf16[256,768]{1,0:T(8,128)(2,1)S(1)}, bf16[256,768]{1,0:T(8,128)(2,1)S(1)}, u32[]{:S(2)}, u32[]{:S(2)}) collective-permute-start(bf16[256,768]{1,0:T(8,128)(2,1)S(1)} %collective-permute-done.20), channel_id=1, source_target_pairs={{0,1},{1,2},{2,3},{3,4},{4,5},{5,6},{6,7},{7,8},{8,9},{9,10},{10,1... | collective-permute-start | bytes 1179656 | tf_op jit(solution)/shard_map/ppermute | solution.py:131
  99.9 43.5 %collective-permute-start.8 = (bf16[256,640]{1,0:T(8,128)(2,1)S(1)}, bf16[256,640]{1,0:T(8,128)(2,1)S(1)}, u32[]{:S(2)}, u32[]{:S(2)}) collective-permute-start(bf16[256,640]{1,0:T(8,128)(2,1)S(1)} %collective-permute-done.7), channel_id=1, source_target_pairs={{0,1},{1,2},{2,3},{3,4},{4,5},{5,6},{6,7},{7,8},{8,9},{9,10},{10,1... | collective-permute-start | bytes 983048 | tf_op jit(solution)/shard_map/ppermute | solution.py:131
  103.4 11.2 %collective-permute-start.16 = (bf16[256,640]{1,0:T(8,128)(2,1)S(1)}, bf16[256,640]{1,0:T(8,128)(2,1)S(1)}, u32[]{:S(2)}, u32[]{:S(2)}) collective-permute-start(bf16[256,640]{1,0:T(8,128)(2,1)S(1)} %collective-permute-done.15), channel_id=1, source_target_pairs={{0,1},{1,2},{2,3},{3,4},{4,5},{5,6},{6,7},{7,8},{8,9},{9,10},{10,1... | collective-permute-start | bytes 983048 | tf_op jit(solution)/shard_map/ppermute | solution.py:131
  107.6 11.2 %collective-permute-start.22 = (bf16[256,768]{1,0:T(8,128)(2,1)S(1)}, bf16[256,768]{1,0:T(8,128)(2,1)S(1)}, u32[]{:S(2)}, u32[]{:S(2)}) collective-permute-start(bf16[256,768]{1,0:T(8,128)(2,1)S(1)} %collective-permute-done.21), channel_id=1, source_target_pairs={{0,1},{1,2},{2,3},{3,4},{4,5},{5,6},{6,7},{7,8},{8,9},{9,10},{10,1... | collective-permute-start | bytes 1179656 | tf_op jit(solution)/shard_map/ppermute | solution.py:131
  114.7 10.2 %collective-permute-start.17 = (bf16[256,640]{1,0:T(8,128)(2,1)S(1)}, bf16[256,640]{1,0:T(8,128)(2,1)S(1)}, u32[]{:S(2)}, u32[]{:S(2)}) collective-permute-start(bf16[256,640]{1,0:T(8,128)(2,1)S(1)} %collective-permute-done.16), channel_id=1, source_target_pairs={{0,1},{1,2},{2,3},{3,4},{4,5},{5,6},{6,7},{7,8},{8,9},{9,10},{10,1... | collective-permute-start | bytes 983048 | tf_op jit(solution)/shard_map/ppermute | solution.py:131
  118.9 10.9 %collective-permute-start.23 = (bf16[256,768]{1,0:T(8,128)(2,1)S(1)}, bf16[256,768]{1,0:T(8,128)(2,1)S(1)}, u32[]{:S(2)}, u32[]{:S(2)}) collective-permute-start(bf16[256,768]{1,0:T(8,128)(2,1)S(1)} %collective-permute-done.22), channel_id=1, source_target_pairs={{0,1},{1,2},{2,3},{3,4},{4,5},{5,6},{6,7},{7,8},{8,9},{9,10},{10,1... | collective-permute-start | bytes 1179656 | tf_op jit(solution)/shard_map/ppermute | solution.py:131
  129.7 10.9 %collective-permute-start.24 = (bf16[256,768]{1,0:T(8,128)(2,1)S(1)}, bf16[256,768]{1,0:T(8,128)(2,1)S(1)}, u32[]{:S(2)}, u32[]{:S(2)}) collective-permute-start(bf16[256,768]{1,0:T(8,128)(2,1)S(1)} %collective-permute-done.23), channel_id=1, source_target_pairs={{0,1},{1,2},{2,3},{3,4},{4,5},{5,6},{6,7},{7,8},{8,9},{9,10},{10,1... | collective-permute-start | bytes 1179656 | tf_op jit(solution)/shard_map/ppermute | solution.py:131
  141.1 24.8 %collective-permute-start.25 = (f32[272,1024]{1,0:T(8,128)S(1)}, f32[272,1024]{1,0:T(8,128)S(1)}, u32[]{:S(2)}, u32[]{:S(2)}) collective-permute-start(f32[272,1024]{1,0:T(8,128)S(1)} %pad_maximum_fusion), channel_id=1, source_target_pairs={{0,16},{16,0},{32,48},{48,32},{64,80},{80,64},{96,112},{112,96},{1... | collective-permute-start | bytes 3342344 | tf_op jit(solution)/shard_map/ppermute | solution.py:134
  143.4 10.2 %collective-permute-start.9 = (bf16[256,640]{1,0:T(8,128)(2,1)S(1)}, bf16[256,640]{1,0:T(8,128)(2,1)S(1)}, u32[]{:S(2)}, u32[]{:S(2)}) collective-permute-start(bf16[256,640]{1,0:T(8,128)(2,1)S(1)} %collective-permute-done.8), channel_id=1, source_target_pairs={{0,1},{1,2},{2,3},{3,4},{4,5},{5,6},{6,7},{7,8},{8,9},{9,10},{10,1... | collective-permute-start | bytes 983048 | tf_op jit(solution)/shard_map/ppermute | solution.py:131
  153.6 10.2 %collective-permute-start.26 = (bf16[256,640]{1,0:T(8,128)(2,1)S(1)}, bf16[256,640]{1,0:T(8,128)(2,1)S(1)}, u32[]{:S(2)}, u32[]{:S(2)}) collective-permute-start(bf16[256,640]{1,0:T(8,128)(2,1)S(1)} %collective-permute-done.9), channel_id=1, source_target_pairs={{0,1},{1,2},{2,3},{3,4},{4,5},{5,6},{6,7},{7,8},{8,9},{9,10},{10,1... | collective-permute-start | bytes 983048 | tf_op jit(solution)/shard_map/ppermute | solution.py:131
  155.6 10.3 %collective-permute-start.27 = (bf16[256,384]{1,0:T(8,128)(2,1)S(1)}, bf16[256,384]{1,0:T(8,128)(2,1)S(1)}, u32[]{:S(2)}, u32[]{:S(2)}) collective-permute-start(bf16[256,384]{1,0:T(8,128)(2,1)S(1)} %slice.58), channel_id=1, source_target_pairs={{0,1},{1,2},{2,3},{3,4},{4,5},{5,6},{6,7},{7,8},{8,9},{9,10},{10,1... | collective-permute-start | bytes 589832 | tf_op jit(solution)/shard_map/ppermute | solution.py:131
  (10 other events, 51.3 us)
